TPU v7x, 32 devices: a whole 2x2x4 slice. The times are simulated.
32 devices in a mesh: sup: 16 (over z, y, x), cls: 2 (over core).
Axes of the slice: x: 2, y: 2, z: 4, core: 2. Of those that a mesh axis runs over, the one named last changes fastest.
Arguments:
- support_feats: bfloat16 [512, 8192], P('sup', 'cls'), may hold values from -6 to 6
- target_feats: bfloat16 [128, 8192], P('sup', 'cls'), may hold values from -6 to 6
- scales: bfloat16 [512], replicated, may hold values from 0.5 to 2
- soft_labels: float32 [512, 5376], P('sup', 'cls'), may hold values from -6 to 6
- target_labels: int32 [128], P('sup'), may hold values from 0 to 5375
Outputs:
- predictions: bfloat16 [128, 5376], P('sup', 'cls')
- hypergrad: float32 [512, 5376], P('sup', 'cls')
All inputs are finite; a program needn't handle non-finite values.
Results may differ from a plain program's by a relative error of at most 0.017.
Values may be sent and summed in bfloat16 or wider, within the bound.
No kernel may reach another device: no remote copies, remote signals or barrier semaphores. Data moves between devices by JAX's collectives and lax.ppermute only.
A program may use at most 64 MiB of HBM per device.

v0:
```python
import jax
import jax.numpy as jnp
from jax import lax
from jax.sharding import PartitionSpec as P

F = 8192
ITERS = 2
RIDGE = 0.05
LABEL_SCALE = 16.0


def conjugate(rhs, kernel):
    result = jnp.zeros_like(rhs)
    resid = rhs
    direction = rhs
    norm_now = jnp.sum(resid * resid, axis=0)
    for step in range(ITERS):
        image = jnp.dot(kernel, direction.astype(jnp.bfloat16), preferred_element_type=jnp.float32)
        curve = jnp.sum(direction * image, axis=0)
        step_size = norm_now / curve
        result = result + step_size * direction
        resid = resid - step_size * image
        norm_next = jnp.sum(resid * resid, axis=0)
        direction = resid + norm_next / norm_now * direction
        norm_now = norm_next
    return result


def local(support_feats, target_feats, scales, soft_labels, target_labels):
    own_support = support_feats.shape[0]
    own_targets = target_feats.shape[0]
    class_count = soft_labels.shape[1]
    sup_count = lax.axis_size("sup")
    support_total = own_support * sup_count
    block_rows = own_targets + own_support
    scale_vec = scales.astype(jnp.float32)
    sup_index = lax.axis_index("sup")
    support_first = sup_index * own_support
    local_rows = jnp.concatenate([target_feats, support_feats], axis=0)
    partial_gram = lax.dot_general(
        local_rows,
        lax.all_gather(support_feats, "sup", axis=0, tiled=True),
        (((1,), (1,)), ((), ())),
        preferred_element_type=jnp.float32,
    )
    own_scales = lax.dynamic_slice_in_dim(scale_vec, support_first, own_support)
    factor_all = jnp.concatenate([jnp.ones((own_targets,), jnp.float32), own_scales])
    share = lax.psum_scatter(partial_gram, "cls", scatter_dimension=0, tiled=True)
    first_row = lax.axis_index("cls") * share.shape[0]
    count = share.shape[0]
    rows = first_row + lax.iota(jnp.int32, count)
    factor = lax.dynamic_slice_in_dim(factor_all, first_row, count)
    support_index = support_first + rows - own_targets
    on_diag = (lax.iota(jnp.int32, support_total)[None, :] == support_index[:, None]) & (
        rows >= own_targets
    )[:, None]
    scaled = share * (factor[:, None] * scale_vec[None, :]) / F
    finished = (scaled + jnp.where(on_diag, RIDGE, 0.0)).astype(jnp.bfloat16)
    kernels = lax.all_gather(finished, ("sup", "cls"), axis=0, tiled=True)
    blocks = kernels.reshape(sup_count, block_rows, support_total)
    cross_kernel = blocks[:, :own_targets].reshape(sup_count * own_targets, support_total)
    support_kernel = blocks[:, own_targets:].reshape(support_total, support_total)
    label_cols = lax.all_to_all(soft_labels, "sup", split_axis=1, concat_axis=0, tiled=True)
    col_width = label_cols.shape[1]
    labels_all = lax.all_gather(target_labels, "sup", axis=0, tiled=True)
    columns = (
        lax.axis_index("cls") * class_count + sup_index * col_width + lax.iota(jnp.int32, col_width)
    )
    alpha = conjugate(label_cols, support_kernel)
    predicted = jnp.dot(
        cross_kernel, alpha.astype(jnp.bfloat16), preferred_element_type=jnp.float32
    )
    onehot = (labels_all[:, None] == columns[None, :]).astype(jnp.float32)
    misfit = (predicted - LABEL_SCALE * onehot).astype(jnp.bfloat16)
    rhs = lax.dot_general(
        cross_kernel, misfit, (((0,), (0,)), ((), ())), preferred_element_type=jnp.float32
    )
    hyper_cols = conjugate(rhs, support_kernel)
    predictions = lax.all_to_all(
        predicted.astype(jnp.bfloat16), "sup", split_axis=0, concat_axis=1, tiled=True
    )
    hypergrad = lax.all_to_all(hyper_cols, "sup", split_axis=0, concat_axis=1, tiled=True)
    return (predictions, hypergrad)


def solution(mesh):
    in_specs = (P("sup", "cls"), P("sup", "cls"), P(), P("sup", "cls"), P("sup"))
    out_specs = (P("sup", "cls"), P("sup", "cls"))
    return jax.shard_map(local, mesh=mesh, in_specs=in_specs, out_specs=out_specs, check_vma=False)
```

profile of v0, /device:TPU:0, one launch (start us, length us, event | category | flops | bytes accessed | tf_op | source)
XLA Modules:
  0.0 184.7 jit_solution(661950115012459254)
XLA Ops:
  7.2 0.0 copy-start
  7.2 0.0 all-gather.3.cloned.1.call-start
  7.2 0.7 all-gather.3.cloned.1.call-update
  7.9 1.7 all_to_all.42
  9.6 1.1 copy.26
  10.7 8.3 %all-to-all-start = ((f32[32,16,168]{2,0,1:T(8,128)}), f32[32,16,168]{2,0,1:T(8,128)S(1)}, u32[]{:S(2)}, u32[]{:S(2)}) async-start(f32[32,16,168]{2,0,1:T(8,128)} %copy.26), calls=%async_computation | async-start | bytes 1048576 | tf_op jit(solution)/shard_map/all_to_all | solution.py:63
  19.1 0.7 convert_element_type.31
  19.8 0.8 dynamic_slice.6
  20.5 1.2 dynamic-slice.5
  22.4 1.2 dynamic-slice
  24.3 0.9 dynamic-update-slice
  25.2 14.8 %all-reduce.1 = s32[128]{0:T(128)S(1)} all-reduce(s32[128]{0:T(128)S(1)} %dynamic-update-slice), channel_id=1, replica_groups=mesh['sup'=16,'cls'=2] {'sup'}, use_global_device_ids=true, to_apply=%add.1 | all-reduce | flops 128 | bytes 1024
  40.0 0.1 pad_dynamic-slice_fusion
  40.1 0.0 all-to-all-done
  40.1 52.1 %all-gather.3.cloned.1.call-done = bf16[512,4096]{1,0:T(8,128)(2,1)} async-done(((bf16[32,4096]{1,0:T(8,128)(2,1)}), bf16[512,4096]{1,0:T(8,128)(2,1)}) %all-gather.3.cloned.1.call-update) | async-done | bytes 4194320 | tf_op jit(solution)/shard_map/all_gather | solution.py:42
  92.2 0.0 copy-done
  92.2 3.6 %fusion.4 = f32[40,512]{1,0:T(8,128)S(1)} fusion(bf16[512,4096]{1,0:T(8,128)(2,1)} %all-gather.3.cloned.1.call-done, bf16[32,4096]{1,0:T(8,128)(2,1)S(1)} %copy-done, bf16[8,4096]{1,0:T(8,128)(2,1)} %param.6), kind=kOutput, calls=%fused_computation.18 | convolution fusion | flops 168427520 | bytes 4603904 | tf_op jit(solution)/shard_map/dot_general | solution.py:40
  95.8 2.9 %fusion = f32[24,512]{1,0:T(8,128)S(1)} fusion(f32[40,512]{1,0:T(8,128)S(1)} %fusion.4), kind=kCustom, calls=%all-reduce-scatter | all-reduce-scatter fusion | flops 24577 | bytes 131584
  98.8 2.3 %collective-permute-start = (f32[4,512]{1,0:T(4,128)S(1)}, f32[4,512]{1,0:T(4,128)S(1)}, u32[]{:S(2)}, u32[]{:S(2)}) collective-permute-start(f32[4,512]{1,0:T(4,128)S(1)} %slice.10), channel_id=1, source_target_pairs={{0,1},{2,3},{4,5},{6,7},{8,9},{10,11},{12,13},{14,15},{16,17},{18,... | collective-permute-start | bytes 24584
  101.0 0.1 fusion.3
  101.1 0.2 copy.27
  101.3 0.5 collective-permute-done
  101.8 0.1 concatenate.8
  102.0 0.1 fusion.29
  102.1 41.4 %all-gather = bf16[32,20,512]{2,1,0:T(8,128)(2,1)S(1)} all-gather(bf16[1,20,512]{2,1,0:T(8,128)(2,1)S(1)} %fusion.29), channel_id=1, replica_groups=mesh['sup'=16,'cls'=2] {'sup','cls'}, dimensions={0}, use_global_device_ids=true | all-gather | bytes 675840 | tf_op jit(solution)/shard_map/all_gather | solution.py:59
  143.4 0.1 reshape.69
  143.6 0.4 multiply_reduce_fusion.4
  144.1 0.2 multiply_reduce_fusion.3
  144.3 0.5 fusion.1
  144.8 0.3 fusion.34
  145.1 0.2 fusion.20
  145.3 0.5 multiply_reduce_fusion.1
  145.8 0.2 multiply_reduce_fusion
  146.0 0.5 fusion.2
  146.5 0.7 copy.31
  147.2 3.5 %all-to-all-start.1 = ((bf16[16,8,168]{2,1,0:T(8,128)(2,1)}), bf16[16,8,168]{2,1,0:T(8,128)(2,1)S(1)}, u32[]{:S(2)}, u32[]{:S(2)}) async-start(bf16[16,8,168]{2,1,0:T(8,128)(2,1)} %bitcast.7), calls=%async_computation.1 | async-start | bytes 131072 | tf_op jit(solution)/shard_map/all_to_all | solution.py:79
  150.8 0.2 multiply_add_fusion
  150.9 1.0 copy.33
  151.9 6.3 %all-to-all-done.1 = bf16[16,8,168]{2,1,0:T(8,128)(2,1)S(1)} async-done(((bf16[16,8,168]{2,1,0:T(8,128)(2,1)}), bf16[16,8,168]{2,1,0:T(8,128)(2,1)S(1)}, u32[]{:S(2)}, u32[]{:S(2)}) %all-to-all-start.1) | async-done | bytes 43040 | tf_op jit(solution)/shard_map/all_to_all | solution.py:79
  158.3 3.6 %all-to-all-start.2 = ((f32[16,32,168]{2,1,0:T(8,128)}), f32[16,32,168]{2,1,0:T(8,128)S(1)}, u32[]{:S(2)}, u32[]{:S(2)}) async-start(f32[16,32,168]{2,1,0:T(8,128)} %bitcast.10), calls=%async_computation.2 | async-start | bytes 1048576 | tf_op jit(solution)/shard_map/all_to_all | solution.py:82
  161.9 0.8 all_to_all.49
  162.6 13.9 %all-to-all-done.2 = f32[16,32,168]{2,1,0:T(8,128)S(1)} async-done(((f32[16,32,168]{2,1,0:T(8,128)}), f32[16,32,168]{2,1,0:T(8,128)S(1)}, u32[]{:S(2)}, u32[]{:S(2)}) %all-to-all-start.2) | async-done | bytes 344096 | tf_op jit(solution)/shard_map/all_to_all | solution.py:82
  176.6 0.3 copy.34
  176.9 1.0 all_to_all.53
  (14 shorter events, 0.2 us)
Async XLA Ops:
  7.2 85.1 %copy-start = (bf16[32,4096]{1,0:T(8,128)(2,1)S(1)}, bf16[32,4096]{1,0:T(8,128)(2,1)}, u32[]{:S(2)}) copy-start(bf16[32,4096]{1,0:T(8,128)(2,1)} %param.5) | copy-start | bytes 786436
  7.2 85.1 %all-gather.3.cloned.1.call-start = ((), (), s32[]{:S(2)}) async-start(), calls=%async_computation.3 | async-start | bytes 4456448 | tf_op jit(solution)/shard_map/all_gather | solution.py:42
  10.7 29.4 %all-to-all-start = ((f32[32,16,168]{2,0,1:T(8,128)}), f32[32,16,168]{2,0,1:T(8,128)S(1)}, u32[]{:S(2)}, u32[]{:S(2)}) async-start(f32[32,16,168]{2,0,1:T(8,128)} %copy.26), calls=%async_computation | async-start | bytes 1048576 | tf_op jit(solution)/shard_map/all_to_all | solution.py:63
  98.8 3.1 %collective-permute-start = (f32[4,512]{1,0:T(4,128)S(1)}, f32[4,512]{1,0:T(4,128)S(1)}, u32[]{:S(2)}, u32[]{:S(2)}) collective-permute-start(f32[4,512]{1,0:T(4,128)S(1)} %slice.10), channel_id=1, source_target_pairs={{0,1},{2,3},{4,5},{6,7},{8,9},{10,11},{12,13},{14,15},{16,17},{18,... | collective-permute-start | bytes 24584
  147.2 11.0 %all-to-all-start.1 = ((bf16[16,8,168]{2,1,0:T(8,128)(2,1)}), bf16[16,8,168]{2,1,0:T(8,128)(2,1)S(1)}, u32[]{:S(2)}, u32[]{:S(2)}) async-start(bf16[16,8,168]{2,1,0:T(8,128)(2,1)} %bitcast.7), calls=%async_computation.1 | async-start | bytes 131072 | tf_op jit(solution)/shard_map/all_to_all | solution.py:79
  158.3 18.3 %all-to-all-start.2 = ((f32[16,32,168]{2,1,0:T(8,128)}), f32[16,32,168]{2,1,0:T(8,128)S(1)}, u32[]{:S(2)}, u32[]{:S(2)}) async-start(f32[16,32,168]{2,1,0:T(8,128)} %bitcast.10), calls=%async_computation.2 | async-start | bytes 1048576 | tf_op jit(solution)/shard_map/all_to_all | solution.py:82
Sparse Core Ops, SparseCore 0:
  10.7 81.4 all-gather.2
where the time goes:
time: 185 us
  waiting for transfers between devices  73.6 us (40%)
  blocking collectives  59.1 us (32%)
  starting transfers between devices  17.7 us (10%)
  between operations  15.5 us (8%)
  local copies, waits for them, and re-layouts  11.3 us (6%)
  matrix products  5.96 us (3%)
    all_gather x1, waiting for transfers between devices, local(): lax.all_gather(support_feats, 'sup', axis=0, tiled=True)  52.1 us
    all_gather x1, blocking collectives, local(): kernels = lax.all_gather(finished, ('sup', 'cls'), axis=0, tiled=True)  41.4 us
    unnamed x2, blocking collectives  17.7 us
    all_to_all x1, waiting for transfers between devices, local(): lax.all_to_all(hyper_cols, 'sup', split_axis=0, concat_axis=1, tiled=True)  13.9 us
    all_to_all x1, starting transfers between devices, local(): lax.all_to_all(soft_labels, 'sup', split_axis=1, concat_axis=0, tiled=True)  8.34 us
    all_to_all x1, waiting for transfers between devices, local(): lax.all_to_all(predicted.astype(jnp.bfloat16), 'sup', split_axis=0, conca...  6.34 us
  transfers between devices with their start and end apart: 5, of which 4 were waited for; matrix products, arithmetic and copies ran while one was open for 4% of the time, Pallas kernels for 0%

commit v1 on v0

--- a/solution.py
+++ b/solution.py
@@ -79,7 +79,10 @@
     predictions = lax.all_to_all(
         predicted.astype(jnp.bfloat16), "sup", split_axis=0, concat_axis=1, tiled=True
     )
-    hypergrad = lax.all_to_all(hyper_cols, "sup", split_axis=0, concat_axis=1, tiled=True)
+    hypergrad = jnp.concatenate(
+        lax.all_to_all(jnp.stack(jnp.split(hyper_cols, lax.axis_size("sup"), axis=0)), "sup", 0, 0),
+        axis=1,
+    )
     return (predictions, hypergrad)
 
 

time: 185 us -> 193 us (1.043)
  local copies, waits for them, and re-layouts: 11.3 us -> 21.6 us
  waiting for transfers between devices: 73.6 us -> 67.9 us
  starting transfers between devices: 17.7 us -> 21 us
    unnamed x8 -> x23, local copies, waits for them, and re-layouts: 3.47 us -> 12.6 us
    all_to_all x1, waiting for transfers between devices: 6.34 us -> 0.01 us  [local(): lax.all_to_all(predicted.astype(jnp.bfloat16), 'sup', split_axis=0, conca...]
    all_to_all x1, starting transfers between devices: 3.57 us -> 6.88 us  [local(): lax.all_to_all(jnp.stack(jnp.split(hyper_cols, lax.axis_size('sup'), axis...]
    another operation x0 -> x18, local copies, waits for them, and re-layouts: none -> 2.13 us  [local(): jnp.stack(jnp.split(hyper_cols, lax.axis_size('sup'), axis=0))]
  transfers between devices with their start and end apart: 5 -> 5, of which waited for: 4 -> 3; matrix products, arithmetic and copies ran while one was open for 4% -> 8% of each run, Pallas kernels for 0% -> 0%
where the time goes in v1:
time: 193 us
  waiting for transfers between devices  67.9 us (35%)
  blocking collectives  59.1 us (31%)
  local copies, waits for them, and re-layouts  21.6 us (11%)
  starting transfers between devices  21 us (11%)
  between operations  15.5 us (8%)
  matrix products  5.95 us (3%)
    all_gather x1, waiting for transfers between devices, local(): lax.all_gather(support_feats, 'sup', axis=0, tiled=True)  52.1 us
    all_gather x1, blocking collectives, local(): kernels = lax.all_gather(finished, ('sup', 'cls'), axis=0, tiled=True)  41.4 us
    unnamed x2, blocking collectives  17.7 us
    all_to_all x1, waiting for transfers between devices, local(): lax.all_to_all(jnp.stack(jnp.split(hyper_cols, lax.axis_size('sup'), axis...  14.5 us
    unnamed x23, local copies, waits for them, and re-layouts  12.6 us
    all_to_all x1, starting transfers between devices, local(): lax.all_to_all(soft_labels, 'sup', split_axis=1, concat_axis=0, tiled=True)  8.34 us
    all_to_all x1, starting transfers between devices, local(): lax.all_to_all(jnp.stack(jnp.split(hyper_cols, lax.axis_size('sup'), axis...  6.88 us
  transfers between devices with their start and end apart: 5, of which 3 were waited for; matrix products, arithmetic and copies ran while one was open for 8% of the time, Pallas kernels for 0%

profile of v1, /device:TPU:0, one launch (start us, length us, event | category | flops | bytes accessed | tf_op | source)
XLA Modules:
  0.0 192.6 jit_solution(3995284523964927333)
XLA Ops:
  7.2 0.7 all-gather.3.cloned.1.call-update
  7.9 1.7 all_to_all.31
  9.6 1.1 copy.48
  10.7 8.3 %all-to-all-start = ((f32[32,16,168]{2,0,1:T(8,128)}), f32[32,16,168]{2,0,1:T(8,128)S(1)}, u32[]{:S(2)}, u32[]{:S(2)}) async-start(f32[32,16,168]{2,0,1:T(8,128)} %copy.48), calls=%async_computation | async-start | bytes 1048576 | tf_op jit(solution)/shard_map/all_to_all | solution.py:63
  19.1 0.7 convert_element_type.31
  19.8 0.8 dynamic_slice.6
  20.5 1.2 dynamic-slice.5
  22.4 1.2 dynamic-slice
  24.3 0.9 dynamic-update-slice
  25.2 14.8 %all-reduce.1 = s32[128]{0:T(128)S(1)} all-reduce(s32[128]{0:T(128)S(1)} %dynamic-update-slice), channel_id=1, replica_groups=mesh['sup'=16,'cls'=2] {'sup'}, use_global_device_ids=true, to_apply=%add.1 | all-reduce | flops 128 | bytes 1024
  40.0 0.1 pad_dynamic-slice_fusion
  40.1 52.1 %all-gather.3.cloned.1.call-done = bf16[512,4096]{1,0:T(8,128)(2,1)} async-done(((bf16[32,4096]{1,0:T(8,128)(2,1)}), bf16[512,4096]{1,0:T(8,128)(2,1)}) %all-gather.3.cloned.1.call-update) | async-done | bytes 4194320 | tf_op jit(solution)/shard_map/all_gather | solution.py:42
  92.2 3.6 %fusion.4 = f32[40,512]{1,0:T(8,128)S(1)} fusion(bf16[512,4096]{1,0:T(8,128)(2,1)} %all-gather.3.cloned.1.call-done, bf16[32,4096]{1,0:T(8,128)(2,1)S(1)} %copy-done, bf16[8,4096]{1,0:T(8,128)(2,1)} %param.6), kind=kOutput, calls=%fused_computation.18 | convolution fusion | flops 168427520 | bytes 4603904 | tf_op jit(solution)/shard_map/dot_general | solution.py:40
  95.8 2.9 %fusion = f32[24,512]{1,0:T(8,128)S(1)} fusion(f32[40,512]{1,0:T(8,128)S(1)} %fusion.4), kind=kCustom, calls=%all-reduce-scatter | all-reduce-scatter fusion | flops 24577 | bytes 131584
  98.8 2.3 %collective-permute-start = (f32[4,512]{1,0:T(4,128)S(1)}, f32[4,512]{1,0:T(4,128)S(1)}, u32[]{:S(2)}, u32[]{:S(2)}) collective-permute-start(f32[4,512]{1,0:T(4,128)S(1)} %slice.10), channel_id=1, source_target_pairs={{0,1},{2,3},{4,5},{6,7},{8,9},{10,11},{12,13},{14,15},{16,17},{18,... | collective-permute-start | bytes 24584
  101.0 0.1 fusion.3
  101.1 0.2 copy.49
  101.3 0.5 collective-permute-done
  101.8 0.1 concatenate.8
  102.0 0.1 fusion.29
  102.1 41.4 %all-gather = bf16[32,20,512]{2,1,0:T(8,128)(2,1)S(1)} all-gather(bf16[1,20,512]{2,1,0:T(8,128)(2,1)S(1)} %fusion.29), channel_id=1, replica_groups=mesh['sup'=16,'cls'=2] {'sup','cls'}, dimensions={0}, use_global_device_ids=true | all-gather | bytes 675840 | tf_op jit(solution)/shard_map/all_gather | solution.py:59
  143.4 0.1 reshape.72
  143.6 0.4 multiply_reduce_fusion.4
  144.1 0.2 multiply_reduce_fusion.3
  144.3 0.5 fusion.1
  144.8 0.3 fusion.34
  145.1 0.2 fusion.20
  145.3 0.5 multiply_reduce_fusion.1
  145.8 0.2 multiply_reduce_fusion
  146.0 0.5 fusion.2
  146.5 0.2 multiply_add_fusion
  146.7 0.3 slice_bitcast_fusion.3
  147.1 0.6 constant_dynamic-update-slice_fusion.15
  147.8 0.1 copy.57
  147.8 0.1 copy.58
  147.9 0.1 copy.59
  148.0 0.1 copy.60
  148.1 0.1 copy.61
  148.4 0.1 copy.65
  148.4 0.1 copy.66
  148.7 0.1 copy.69
  148.7 0.1 copy.70
  148.8 0.8 copy.53
  149.6 3.5 %all-to-all-start.1 = ((bf16[16,8,168]{2,1,0:T(8,128)(2,1)}), bf16[16,8,168]{2,1,0:T(8,128)(2,1)S(1)}, u32[]{:S(2)}, u32[]{:S(2)}) async-start(bf16[16,8,168]{2,1,0:T(8,128)(2,1)} %bitcast.7), calls=%async_computation.1 | async-start | bytes 131072 | tf_op jit(solution)/shard_map/all_to_all | solution.py:79
  153.1 0.6 constant_dynamic-update-slice_fusion.14
  153.7 0.6 constant_dynamic-update-slice_fusion.13
  154.3 0.6 constant_dynamic-update-slice_fusion.12
  154.9 0.6 constant_dynamic-update-slice_fusion.11
  155.5 0.6 constant_dynamic-update-slice_fusion.10
  156.1 0.6 constant_dynamic-update-slice_fusion.9
  156.7 0.6 constant_dynamic-update-slice_fusion.8
  157.3 0.6 constant_dynamic-update-slice_fusion.7
  157.9 0.6 constant_dynamic-update-slice_fusion.6
  158.5 0.6 constant_dynamic-update-slice_fusion.5
  159.1 0.6 constant_dynamic-update-slice_fusion.4
  159.8 0.6 constant_dynamic-update-slice_fusion.3
  160.4 0.6 constant_dynamic-update-slice_fusion.2
  161.0 0.6 constant_dynamic-update-slice_fusion.1
  161.6 0.6 constant_dynamic-update-slice_fusion
  162.2 6.9 %all-to-all-start.2 = ((f32[16,32,168]{2,1,0:T(8,128)}), f32[16,32,168]{2,1,0:T(8,128)S(1)}, u32[]{:S(2)}, u32[]{:S(2)}) async-start(f32[16,32,168]{2,1,0:T(8,128)} %constant_dynamic-update-slice_fusion), calls=%async_computation.2 | async-start | bytes 1048576 | tf_op jit(solution)/shard_map/all_to_all | solution.py:83
  169.1 0.8 all_to_all.38
  169.8 14.5 %all-to-all-done.2 = f32[16,32,168]{2,1,0:T(8,128)S(1)} async-done(((f32[16,32,168]{2,1,0:T(8,128)}), f32[16,32,168]{2,1,0:T(8,128)S(1)}, u32[]{:S(2)}, u32[]{:S(2)}) %all-to-all-start.2) | async-done | bytes 344096 | tf_op jit(solution)/shard_map/all_to_all | solution.py:83
  184.4 0.3 copy.71
  184.7 1.0 reshape.76
  (26 shorter events, 0.7 us)
Async XLA Ops:
  7.2 85.1 %copy-start = (bf16[32,4096]{1,0:T(8,128)(2,1)S(1)}, bf16[32,4096]{1,0:T(8,128)(2,1)}, u32[]{:S(2)}) copy-start(bf16[32,4096]{1,0:T(8,128)(2,1)} %param.5) | copy-start | bytes 786436
  7.2 85.1 %all-gather.3.cloned.1.call-start = ((), (), s32[]{:S(2)}) async-start(), calls=%async_computation.3 | async-start | bytes 4456448 | tf_op jit(solution)/shard_map/all_gather | solution.py:42
  10.7 29.4 %all-to-all-start = ((f32[32,16,168]{2,0,1:T(8,128)}), f32[32,16,168]{2,0,1:T(8,128)S(1)}, u32[]{:S(2)}, u32[]{:S(2)}) async-start(f32[32,16,168]{2,0,1:T(8,128)} %copy.48), calls=%async_computation | async-start | bytes 1048576 | tf_op jit(solution)/shard_map/all_to_all | solution.py:63
  98.8 3.1 %collective-permute-start = (f32[4,512]{1,0:T(4,128)S(1)}, f32[4,512]{1,0:T(4,128)S(1)}, u32[]{:S(2)}, u32[]{:S(2)}) collective-permute-start(f32[4,512]{1,0:T(4,128)S(1)} %slice.10), channel_id=1, source_target_pairs={{0,1},{2,3},{4,5},{6,7},{8,9},{10,11},{12,13},{14,15},{16,17},{18,... | collective-permute-start | bytes 24584
  149.6 12.6 %all-to-all-start.1 = ((bf16[16,8,168]{2,1,0:T(8,128)(2,1)}), bf16[16,8,168]{2,1,0:T(8,128)(2,1)S(1)}, u32[]{:S(2)}, u32[]{:S(2)}) async-start(bf16[16,8,168]{2,1,0:T(8,128)(2,1)} %bitcast.7), calls=%async_computation.1 | async-start | bytes 131072 | tf_op jit(solution)/shard_map/all_to_all | solution.py:79
  162.2 22.2 %all-to-all-start.2 = ((f32[16,32,168]{2,1,0:T(8,128)}), f32[16,32,168]{2,1,0:T(8,128)S(1)}, u32[]{:S(2)}, u32[]{:S(2)}) async-start(f32[16,32,168]{2,1,0:T(8,128)} %constant_dynamic-update-slice_fusion), calls=%async_computation.2 | async-start | bytes 1048576 | tf_op jit(solution)/shard_map/all_to_all | solution.py:83
Sparse Core Ops, SparseCore 0:
  10.7 81.4 all-gather.2
